TPU v7x, 256 devices: a whole 4x4x8 slice. The times are simulated.
256 devices in a mesh: param: 16 (over z, core), ex: 16 (over x, y).
Axes of the slice: x: 4, y: 4, z: 8, core: 2. Of those that a mesh axis runs over, the one named last changes fastest.
Arguments:
- query_acts: bfloat16 [16, 256, 16, 4096], P(None, 'ex', None, 'param'), may hold values from -6 to 6
- query_grads: bfloat16 [16, 256, 16, 4096], P(None, 'ex', None, 'param'), may hold values from -6 to 6
- train_acts: bfloat16 [16, 512, 16, 4096], P(None, 'ex', None, 'param'), as said below
- train_grads: bfloat16 [16, 512, 16, 4096], P(None, 'ex', None, 'param'), as said below
- input_projection: bfloat16 [4096, 128], P('param'), as said below
- proj_out: bfloat16 [4096, 64], P('param'), as said below
- query_clusters: int32 [16, 256], P('param'), may hold values from 0 to 127
- train_clusters: int32 [16, 512], P(None, 'ex'), may hold values from 0 to 127
- pair_mask: int32 [128, 128], replicated, may hold values 0 or 1
Outputs:
- scores: float32 [16, 256, 16, 512], P('param', None, None, 'ex')
- cluster_scores: float32 [16, 256, 128], P('param', 'ex')
Inputs may be any that keep to these rules, and one draw needn't show every extreme that they name: `train_acts`: token features whose scales differ from token to token and from example to example. `train_grads`: token gradients whose scales differ from example to example. `input_projection`: random projection columns of differing scales. `proj_out`: random projection columns of differing scales.
All inputs are finite; a program needn't handle non-finite values.
Results may differ from a plain program's by a relative error of at most 0.022.
The roundings to bfloat16 on the way count: a program that leaves them out, or rounds other values in their place, can miss the bound.
Values may be sent and summed in bfloat16 or wider, within the bound.
A program may use at most 128 MiB of HBM per device.

v0:
```python
import math
import jax
import jax.numpy as jnp
from jax import lax
from jax.sharding import PartitionSpec as P


def inverse_of(gram, count):
    mean = gram / count
    size = gram.shape[0]
    damping = 0.1 * jnp.trace(mean) / size
    identity = jnp.eye(size, dtype=gram.dtype)
    factor = jnp.linalg.cholesky(mean + damping * identity)
    return jax.scipy.linalg.cho_solve((factor, True), identity)


def form_grads(part_out, part_in):
    examples = part_out.shape[0]
    grad = jnp.einsum("tkr,tks->trs", part_out, part_in, preferred_element_type=jnp.float32)
    return grad.reshape(examples, -1).astype(jnp.bfloat16)


def shards(
    query_acts,
    query_grads,
    train_acts,
    train_grads,
    input_projection,
    proj_out,
    query_clusters,
    train_clusters,
    pair_mask,
):
    group_batches = train_acts.shape[0]
    query_rows = query_acts.shape[1]
    train_rows = train_acts.shape[1]
    tokens = train_acts.shape[2]
    width_in = input_projection.shape[1]
    width_out = proj_out.shape[1]
    clusters = pair_mask.shape[0]
    pieces = []
    for acts, grads in ((query_acts, query_grads), (train_acts, train_grads)):
        lead = acts.shape[:3]
        flat_acts = acts.reshape(-1, acts.shape[3])
        flat_grads = grads.reshape(-1, grads.shape[3])
        joined = jnp.concatenate(
            [
                jnp.dot(flat_acts, input_projection, preferred_element_type=jnp.float32),
                jnp.dot(flat_grads, proj_out, preferred_element_type=jnp.float32),
            ],
            axis=1,
        )
        pieces.append(joined.reshape(lead + (width_in + width_out,)))
    projected = lax.psum_scatter(
        jnp.concatenate(pieces, axis=1), "param", scatter_dimension=0, tiled=True
    ).astype(jnp.bfloat16)
    factors = projected[0]
    query_in = factors[:query_rows, :, :width_in]
    query_output_side = factors[:query_rows, :, width_in:]
    train_in = factors[query_rows:, :, :width_in]
    train_out = factors[query_rows:, :, width_in:]
    flat_in = train_in.reshape(-1, width_in)
    flat_out = train_out.reshape(-1, width_out)
    gram_in = jnp.dot(flat_in.T, flat_in, preferred_element_type=jnp.float32)
    gram_out = jnp.dot(flat_out.T, flat_out, preferred_element_type=jnp.float32)
    gram_in, gram_out = lax.psum((gram_in, gram_out), ("param", "ex"))
    total_train = group_batches * train_rows * lax.axis_size("ex")
    count = float(total_train * tokens)
    inv_in = inverse_of(gram_in, count)
    inv_out = inverse_of(gram_out, count)
    preconditioned_input = jnp.dot(
        query_in.reshape(-1, width_in).astype(jnp.float32), inv_in, precision=lax.Precision.HIGHEST
    ).reshape(query_rows, tokens, width_in)
    preconditioned_output = jnp.dot(
        query_output_side.reshape(-1, width_out).astype(jnp.float32),
        inv_out,
        precision=lax.Precision.HIGHEST,
    ).reshape(query_rows, tokens, width_out)
    query_before_preconditioning = jnp.einsum(
        "bui,bux->bix", preconditioned_output, preconditioned_input, precision=lax.Precision.HIGHEST
    )
    query_before_preconditioning = query_before_preconditioning.reshape(query_rows, -1).astype(
        jnp.bfloat16
    )
    trains = lax.all_gather(form_grads(train_out, train_in), "param", axis=0, tiled=True)
    cluster_ids = jnp.arange(clusters, dtype=jnp.int32)
    train_onehot = train_clusters.reshape(-1)[:, None] == cluster_ids[None, :]
    train_side = train_onehot.astype(jnp.bfloat16)
    mask_values = pair_mask.astype(jnp.bfloat16)
    scale = 1.0 / (tokens * math.sqrt(width_in * width_out))
    contract = (((1,), (1,)), ((), ()))
    ids = query_clusters[0]
    query_onehot = (ids[:, None] == cluster_ids[None, :]).astype(jnp.bfloat16)
    picked = jnp.dot(query_onehot, mask_values, preferred_element_type=jnp.float32).astype(
        jnp.bfloat16
    )
    allowed = lax.dot_general(picked, train_side, contract, preferred_element_type=jnp.float32)
    raw = lax.dot_general(
        lax.all_gather(query_before_preconditioning, "ex", axis=0, tiled=True),
        trains,
        contract,
        preferred_element_type=jnp.float32,
    )
    scores = raw * scale * allowed
    partial_value = jnp.dot(
        scores, train_onehot.astype(jnp.float32), precision=lax.Precision.HIGHEST
    ) * math.sqrt(clusters / total_train)
    summed = lax.psum_scatter(
        partial_value.astype(jnp.bfloat16), "ex", scatter_dimension=0, tiled=True
    ).astype(jnp.float32)
    all_queries = scores.shape[0]
    return (
        scores.reshape(1, all_queries, group_batches, train_rows),
        summed.reshape(1, summed.shape[0], clusters),
    )


def solution(mesh):
    return jax.shard_map(
        shards,
        mesh=mesh,
        in_specs=(
            P(None, "ex", None, "param"),
            P(None, "ex", None, "param"),
            P(None, "ex", None, "param"),
            P(None, "ex", None, "param"),
            P("param", None),
            P("param", None),
            P("param", None),
            P(None, "ex"),
            P(),
        ),
        out_specs=(P("param", None, None, "ex"), P("param", "ex", None)),
        check_vma=False,
    )
```

profile of v0, /device:TPU:2, one launch (start us, length us, event | category | flops | bytes accessed | tf_op | source)
XLA Modules:
  0.0 642.3 jit_solution(12987489176357474776)
XLA Ops:
  7.2 0.0 copy-start
  7.2 0.0 reduce-scatter.2.cloned.1.call-start
  7.2 3.8 fusion.27
  11.1 1.4 fusion.28
  12.5 3.1 pad_maximum_fusion.1
  15.6 8.4 %copy.28 = f32[8192,192]{1,0:T(8,128)} copy(f32[8192,192]{0,1:T(8,128)} %pad_maximum_fusion.1) | data formatting | bytes 12582912 | tf_op jit(solution)/shard_map/concatenate | solution.py:46
  24.1 13.1 %copy.30 = f32[16,32,16,192]{3,1,2,0:T(8,128)} copy(f32[16,32,16,192]{3,2,1,0:T(8,128)} %bitcast.70) | data formatting | bytes 12582912 | tf_op jit(solution)/shard_map/reshape | solution.py:53
  37.2 0.8 fusion.25
  38.0 0.8 copy-done.3
  38.7 0.7 fusion.26
  39.5 2.0 pad_maximum_fusion.2
  41.4 5.1 copy.27
  46.6 7.4 %copy.29 = f32[16,16,16,192]{3,1,2,0:T(8,128)} copy(f32[16,16,16,192]{3,2,1,0:T(8,128)} %bitcast.71) | data formatting | bytes 6291456 | tf_op jit(solution)/shard_map/reshape | solution.py:53
  54.0 11.0 %pad_maximum_fusion = f32[16,48,16,192]{3,1,2,0:T(8,128)} fusion(f32[16,32,16,192]{3,1,2,0:T(8,128)} %copy.30, f32[16,16,16,192]{3,1,2,0:T(8,128)} %copy.29), kind=kLoop, calls=%fused_computation | loop fusion | flops 2359296 | bytes 18874368 | tf_op jit(solution)/shard_map/concatenate | solution.py:55
  65.0 0.0 reduce-scatter.2.cloned.1.call-update
  65.0 0.0 copy-start.7
  65.0 0.0 all-reduce.4.cloned.1.call-start
  65.1 82.4 %reduce-scatter.2.cloned.1.call-done = f32[1,48,16,192]{3,1,2,0:T(8,128)} async-done(((f32[16,48,16,192]{3,1,2,0:T(8,128)}), f32[1,48,16,192]{3,1,2,0:T(8,128)}) %reduce-scatter.2.cloned.1.call-update) | async-done | bytes 589840 | tf_op jit(solution)/shard_map/reduce_scatter | solution.py:54
  147.4 1.2 convert_bitcast_fusion
  148.6 0.9 convolution_bitcast_fusion.1
  149.5 0.2 convolution_bitcast_fusion.3
  149.7 0.0 all-reduce.4.cloned.1.call-update
  149.7 0.0 all-gather.3.cloned.1.call-start
  149.8 75.2 %psum.14 = f32[64,64]{1,0:T(8,128)S(1)} all-reduce(f32[64,64]{1,0:T(8,128)S(1)} %convolution_bitcast_fusion.3), channel_id=1, replica_groups=mesh['param'=16,'ex'=16] {'param','ex'}, use_global_device_ids=true, to_apply=%region_1.0 | all-reduce | flops 4096 | bytes 32768 | tf_op jit(solution)/shard_map/psum | solution.py:66
  225.0 0.6 select_reduce_fusion.3
  226.3 0.1 copy.31
  226.4 5.8 cholesky.33
  232.3 0.6 compare_reduce_fusion.1
  232.9 0.7 fusion.16
  233.6 4.9 custom-call.20
  238.5 0.2 fusion.18
  238.7 0.2 convolution_bitcast_fusion.2
  238.9 0.2 fusion.12
  239.1 155.0 %all-reduce.4.cloned.1.call-done = f32[128,128]{1,0:T(8,128)} async-done(((f32[128,128]{1,0:T(8,128)}), f32[128,128]{1,0:T(8,128)}) %all-reduce.4.cloned.1.call-update) | async-done | bytes 65552 | tf_op jit(solution)/shard_map/psum | solution.py:66
  394.1 1.5 select_reduce_fusion.1
  396.3 0.9 select_add_fusion
  397.1 0.1 copy.33
  397.2 0.9 fusion.9
  398.1 11.7 %cholesky.68 = f32[128,128]{1,0:T(8,128)S(1)} custom-call(f32[128,128]{1,0:T(8,128)S(1)} %fusion.9), custom_call_target="Cholesky" | custom-call | tf_op jit(solution)/shard_map/jit(cholesky)/cholesky | solution.py:13
  409.8 0.6 compare_reduce_fusion
  410.5 0.7 fusion.5
  411.1 9.8 %custom-call.21 = f32[1,128,128]{1,2,0:T(8,128)S(1)} custom-call(f32[1,128,128]{2,1,0:T(8,128)S(1)} %fusion.5), custom_call_target="InvertDiagBlocksLowerTriangular" | custom-call | tf_op jit(solution)/shard_map/jit(_cho_solve)/triangular_solve | solution.py:14
  420.9 0.2 fusion.7
  421.2 0.2 convolution_bitcast_fusion
  421.4 0.2 fusion.10
  421.6 1.0 convolution_convert_fusion.1
  422.6 0.9 copy.51
  423.5 0.0 all-gather.3.cloned.1.call-update
  423.6 0.0 all-gather.5.cloned.1.call-start
  423.7 0.3 convolution_convert_fusion
  424.0 1.1 copy.50
  425.1 0.0 all-gather.5.cloned.1.call-update
  425.2 0.3 all-reduce.6.cloned.1.call-start
  425.5 0.1 eq.40
  425.5 51.9 %all-gather.3.cloned.1.call-done = bf16[256,8192]{1,0:T(8,128)(2,1)} async-done(((bf16[16,8192]{1,0:T(8,128)(2,1)}), bf16[256,8192]{1,0:T(8,128)(2,1)}) %all-gather.3.cloned.1.call-update) | async-done | bytes 4194320 | tf_op jit(solution)/shard_map/all_gather | solution.py:99
  477.5 57.9 %all-gather.5.cloned.1.call-done = bf16[512,8192]{1,0:T(8,128)(2,1)} async-done(((bf16[32,8192]{1,0:T(8,128)(2,1)}), bf16[512,8192]{1,0:T(8,128)(2,1)}) %all-gather.5.cloned.1.call-update) | async-done | bytes 8388624 | tf_op jit(solution)/shard_map/all_gather | solution.py:85
  535.3 7.2 %convolution_multiply_fusion.1 = f32[256,512]{1,0:T(8,128)S(1)} fusion(bf16[256,8192]{1,0:T(8,128)(2,1)} %all-gather.3.cloned.1.call-done, bf16[512,8192]{1,0:T(8,128)(2,1)} %all-gather.5.cloned.1.call-done), kind=kOutput, calls=%fused_computation.5 | convolution fusion | flops 2147614720 | bytes 13107200 | tf_op jit(solution)/shard_map/dot_general | solution.py:98
  542.5 0.4 convolution_multiply_fusion
  542.9 1.1 fusion
  544.0 0.0 all-reduce.6.cloned.1.call-update
  544.1 0.6 dynamic-slice
  545.3 1.0 copy.37
  546.3 88.2 %all-reduce.6.cloned.1.call-done = bf16[256,128]{1,0:T(8,128)(2,1)} async-done(((bf16[256,128]{1,0:T(8,128)(2,1)}), bf16[256,128]{1,0:T(8,128)(2,1)}) %all-reduce.6.cloned.1.call-update) | async-done | bytes 65552
  634.5 1.3 bitcast_convert_fusion
  (25 shorter events, 0.2 us)
Async XLA Ops:
  7.2 30.0 %copy-start = (bf16[16,16,16,256]{3,2,1,0:T(8,128)(2,1)S(1)}, bf16[16,16,16,256]{3,2,1,0:T(8,128)(2,1)}, u32[]{:S(2)}) copy-start(bf16[16,16,16,256]{3,2,1,0:T(8,128)(2,1)} %param.9) | copy-start | bytes 6291460
  7.2 140.3 %reduce-scatter.2.cloned.1.call-start = ((), (), s32[]{:S(2)}) async-start(), calls=%async_computation.1 | async-start | bytes 13369344 | tf_op jit(solution)/shard_map/reduce_scatter | solution.py:54
  7.2 3.9 copy-start.2
  7.2 3.9 copy-start.5
  24.1 13.1 %copy-start.4 = (bf16[256,128]{1,0:T(8,128)(2,1)S(1)}, bf16[256,128]{1,0:T(8,128)(2,1)}, u32[]{:S(2)}) copy-start(bf16[256,128]{1,0:T(8,128)(2,1)} %param.13) | copy-start | bytes 196612
  37.1 1.6 copy-start.3
  65.0 360.5 %copy-start.7 = (s32[16,32]{1,0:T(8,128)S(1)}, s32[16,32]{1,0:T(8,128)}, u32[]{:S(2)}) copy-start(s32[16,32]{1,0:T(8,128)} %param.16) | copy-start | bytes 6148
  65.0 329.1 %all-reduce.4.cloned.1.call-start = ((), (), s32[]{:S(2)}) async-start(), calls=%async_computation.2 | async-start | bytes 131072 | tf_op jit(solution)/shard_map/psum | solution.py:66
  149.7 327.7 %all-gather.3.cloned.1.call-start = ((), (), s32[]{:S(2)}) async-start(), calls=%async_computation.3 | async-start | bytes 4456448 | tf_op jit(solution)/shard_map/all_gather | solution.py:99
  423.6 111.8 %all-gather.5.cloned.1.call-start = ((), (), s32[]{:S(2)}) async-start(), calls=%async_computation.4 | async-start | bytes 8912896 | tf_op jit(solution)/shard_map/all_gather | solution.py:85
  425.2 209.3 %all-reduce.6.cloned.1.call-start = ((), (), s32[]{:S(2)}) async-start(), calls=%async_computation.5 | async-start | bytes 131072
  425.5 117.0 %copy-start.6 = (s32[128,128]{1,0:T(8,128)S(1)}, s32[128,128]{1,0:T(8,128)}, u32[]{:S(2)}) copy-start(s32[128,128]{1,0:T(8,128)} %param.17) | copy-start | bytes 196612
  425.5 117.0 %copy-start.8 = (s32[1,256]{1,0:T(1,128)S(1)}, s32[1,256]{1,0:T(1,128)}, u32[]{:S(2)}) copy-start(s32[1,256]{1,0:T(1,128)} %param.15) | copy-start | bytes 3076
  425.5 118.5 %copy-start.9 = (u32[256]{0:T(256)S(1)}, u32[256]{0:T(256)}, u32[]{:S(2)}) copy-start(u32[256]{0:T(256)} %constant.124) | copy-start | bytes 3076
  535.3 100.4 %copy-start.1 = (bf16[16,16,16,256]{3,2,1,0:T(8,128)(2,1)S(1)}, bf16[16,16,16,256]{3,2,1,0:T(8,128)(2,1)}, u32[]{:S(2)}) copy-start(bf16[16,16,16,256]{3,2,1,0:T(8,128)(2,1)} %param.9) | copy-start | bytes 6291460
Sparse Core Ops, SparseCore 0:
  65.1 82.2 reduce-scatter.1
  153.5 240.5 all-reduce.3
  423.7 53.7 all-gather.2
  479.7 55.5 all-gather.4
  544.2 90.2 all-reduce.5
where the time goes:
time: 643 us; the launch traced here: 642 us
  waiting for transfers between devices  436 us (68%)
  blocking collectives  75.2 us (12%)
  other arithmetic  57.3 us (9%)
  local copies, waits for them, and re-layouts  38.8 us (6%)
  matrix products  19.1 us (3%)
  between operations  16 us (2%)
    psum x1, waiting for transfers between devices, shards(): gram_in, gram_out = lax.psum((gram_in, gram_out), ('param', 'ex'))  155 us
    unnamed x6, waiting for transfers between devices  88.3 us
    reduce_scatter x1, waiting for transfers between devices, shards(): lax.psum_scatter(jnp.concatenate(pieces, axis=1), 'param', scatter_dimens...  82.4 us
    psum x1, blocking collectives, shards(): gram_in, gram_out = lax.psum((gram_in, gram_out), ('param', 'ex'))  75.2 us
    all_gather x1, waiting for transfers between devices, shards(): lax.all_gather(form_grads(train_out, train_in), 'param', axis=0, tiled=True)  57.9 us
    all_gather x1, waiting for transfers between devices, shards(): lax.all_gather(query_before_preconditioning, 'ex', axis=0, tiled=True)  51.9 us
    reshape x2, local copies, waits for them, and re-layouts, shards(): pieces.append(joined.reshape(lead + (width_in + width_out,)))  20.5 us
    another operation x6, other arithmetic, inverse_of(): factor = jnp.linalg.cholesky(mean + damping * identity)  18.9 us
  transfers between devices with their start and end apart: 5, of which 5 were waited for; matrix products, arithmetic and copies ran while one was open for 3% of the time, Pallas kernels for 0%

commit v1 on v0

--- a/solution.py
+++ b/solution.py
@@ -63,7 +63,7 @@
     flat_out = train_out.reshape(-1, width_out)
     gram_in = jnp.dot(flat_in.T, flat_in, preferred_element_type=jnp.float32)
     gram_out = jnp.dot(flat_out.T, flat_out, preferred_element_type=jnp.float32)
-    gram_in, gram_out = lax.psum((gram_in, gram_out), ("param", "ex"))
+    gram_in, gram_out = lax.psum(lax.psum((gram_in, gram_out), "param"), "ex")
     total_train = group_batches * train_rows * lax.axis_size("ex")
     count = float(total_train * tokens)
     inv_in = inverse_of(gram_in, count)

time: 643 us -> 623 us (0.969)
  waiting for transfers between devices: 436 us -> 375 us
  blocking collectives: 75.2 us -> 115 us
    psum x1 -> x2, waiting for transfers between devices: 155 us -> 92.3 us  [shards(): gram_in, gram_out = lax.psum(lax.psum((gram_in, gram_out), 'param'), 'ex')]
    psum x1 -> x2, blocking collectives: 75.2 us -> 115 us  [shards(): gram_in, gram_out = lax.psum(lax.psum((gram_in, gram_out), 'param'), 'ex')]
    unnamed x6 -> x7, waiting for transfers between devices: 88.3 us -> 88.3 us
  transfers between devices with their start and end apart: 5 -> 6, of which waited for: 5 -> 5; matrix products, arithmetic and copies ran while one was open for 3% -> 3% of each run, Pallas kernels for 0% -> 0%
where the time goes in v1:
time: 623 us
  waiting for transfers between devices  375 us (60%)
  blocking collectives  115 us (18%)
  other arithmetic  57.3 us (9%)
  local copies, waits for them, and re-layouts  38.8 us (6%)
  matrix products  19.1 us (3%)
  between operations  16.4 us (3%)
    psum x2, blocking collectives, shards(): gram_in, gram_out = lax.psum(lax.psum((gram_in, gram_out), 'param'), 'ex')  115 us
    psum x2, waiting for transfers between devices, shards(): gram_in, gram_out = lax.psum(lax.psum((gram_in, gram_out), 'param'), 'ex')  92.3 us
    unnamed x7, waiting for transfers between devices  88.3 us
    reduce_scatter x1, waiting for transfers between devices, shards(): lax.psum_scatter(jnp.concatenate(pieces, axis=1), 'param', scatter_dimens...  82.4 us
    all_gather x1, waiting for transfers between devices, shards(): lax.all_gather(form_grads(train_out, train_in), 'param', axis=0, tiled=True)  57.9 us
    all_gather x1, waiting for transfers between devices, shards(): lax.all_gather(query_before_preconditioning, 'ex', axis=0, tiled=True)  54.6 us
    reshape x2, local copies, waits for them, and re-layouts, shards(): pieces.append(joined.reshape(lead + (width_in + width_out,)))  20.5 us
    another operation x6, other arithmetic, inverse_of(): factor = jnp.linalg.cholesky(mean + damping * identity)  18.9 us
  transfers between devices with their start and end apart: 6, of which 5 were waited for; matrix products, arithmetic and copies ran while one was open for 3% of the time, Pallas kernels for 0%

profile of v1, /device:TPU:2, one launch (start us, length us, event | category | flops | bytes accessed | tf_op | source)
XLA Modules:
  0.0 622.6 jit_solution(4170196785475116192)
XLA Ops:
  7.2 0.0 reduce-scatter.2.cloned.1.call-start
  7.2 3.8 fusion.27
  11.1 1.4 fusion.28
  12.5 3.1 pad_maximum_fusion.1
  15.6 8.4 %copy.28 = f32[8192,192]{1,0:T(8,128)} copy(f32[8192,192]{0,1:T(8,128)} %pad_maximum_fusion.1) | data formatting | bytes 12582912 | tf_op jit(solution)/shard_map/concatenate | solution.py:46
  24.1 13.1 %copy.30 = f32[16,32,16,192]{3,1,2,0:T(8,128)} copy(f32[16,32,16,192]{3,2,1,0:T(8,128)} %bitcast.70) | data formatting | bytes 12582912 | tf_op jit(solution)/shard_map/reshape | solution.py:53
  37.2 0.8 fusion.25
  38.0 0.8 copy-done.3
  38.7 0.7 fusion.26
  39.5 2.0 pad_maximum_fusion.2
  41.4 5.1 copy.27
  46.6 7.4 %copy.29 = f32[16,16,16,192]{3,1,2,0:T(8,128)} copy(f32[16,16,16,192]{3,2,1,0:T(8,128)} %bitcast.71) | data formatting | bytes 6291456 | tf_op jit(solution)/shard_map/reshape | solution.py:53
  54.0 11.0 %pad_maximum_fusion = f32[16,48,16,192]{3,1,2,0:T(8,128)} fusion(f32[16,32,16,192]{3,1,2,0:T(8,128)} %copy.30, f32[16,16,16,192]{3,1,2,0:T(8,128)} %copy.29), kind=kLoop, calls=%fused_computation | loop fusion | flops 2359296 | bytes 18874368 | tf_op jit(solution)/shard_map/concatenate | solution.py:55
  65.0 0.0 all-reduce.5.cloned.1.call-start
  65.1 82.4 %reduce-scatter.2.cloned.1.call-done = f32[1,48,16,192]{3,1,2,0:T(8,128)} async-done(((f32[16,48,16,192]{3,1,2,0:T(8,128)}), f32[1,48,16,192]{3,1,2,0:T(8,128)}) %reduce-scatter.2.cloned.1.call-update) | async-done | bytes 589840 | tf_op jit(solution)/shard_map/reduce_scatter | solution.py:54
  147.4 1.2 convert_bitcast_fusion
  148.6 0.9 convolution_bitcast_fusion.1
  149.5 0.2 convolution_bitcast_fusion.3
  149.7 0.0 all-reduce.5.cloned.1.call-update
  149.7 0.0 all-reduce.7.cloned.1.call-start
  149.8 47.0 %psum.28 = f32[64,64]{1,0:T(8,128)S(1)} all-reduce(f32[64,64]{1,0:T(8,128)S(1)} %convolution_bitcast_fusion.3), channel_id=1, replica_groups=mesh['param'=16,'ex'=16] {'param'}, use_global_device_ids=true, to_apply=%region_1.0 | all-reduce | flops 4096 | bytes 32768 | tf_op jit(solution)/shard_map/psum | solution.py:66
  196.8 68.2 %psum.29 = f32[64,64]{1,0:T(8,128)S(1)} all-reduce(f32[64,64]{1,0:T(8,128)S(1)} %psum.28), channel_id=1, replica_groups=mesh['param'=16,'ex'=16] {'ex'}, use_global_device_ids=true, to_apply=%region_2.0 | all-reduce | flops 4096 | bytes 32768 | tf_op jit(solution)/shard_map/psum | solution.py:66
  265.0 0.6 select_reduce_fusion.3
  266.2 0.1 copy.31
  266.3 5.8 cholesky.33
  272.2 0.6 compare_reduce_fusion.1
  272.9 0.7 fusion.16
  273.5 4.9 custom-call.20
  278.4 0.2 fusion.18
  278.7 0.2 convolution_bitcast_fusion.2
  278.8 0.0 all-reduce.5.cloned.1.call-done
  278.9 0.0 all-reduce.7.cloned.1.call-update
  278.9 0.3 all-gather.3.cloned.1.call-start
  279.2 0.2 fusion.12
  279.4 92.3 %all-reduce.7.cloned.1.call-done = f32[128,128]{1,0:T(8,128)} async-done(((f32[128,128]{1,0:T(8,128)}), f32[128,128]{1,0:T(8,128)}) %all-reduce.7.cloned.1.call-update) | async-done | bytes 65552 | tf_op jit(solution)/shard_map/psum | solution.py:66
  371.7 1.5 select_reduce_fusion.1
  373.8 0.9 select_add_fusion
  374.7 0.1 copy.33
  374.8 0.9 fusion.9
  375.6 11.7 %cholesky.68 = f32[128,128]{1,0:T(8,128)S(1)} custom-call(f32[128,128]{1,0:T(8,128)S(1)} %fusion.9), custom_call_target="Cholesky" | custom-call | tf_op jit(solution)/shard_map/jit(cholesky)/cholesky | solution.py:13
  387.4 0.6 compare_reduce_fusion
  388.0 0.7 fusion.5
  388.7 9.8 %custom-call.21 = f32[1,128,128]{1,2,0:T(8,128)S(1)} custom-call(f32[1,128,128]{2,1,0:T(8,128)S(1)} %fusion.5), custom_call_target="InvertDiagBlocksLowerTriangular" | custom-call | tf_op jit(solution)/shard_map/jit(_cho_solve)/triangular_solve | solution.py:14
  398.5 0.2 fusion.7
  398.8 0.2 convolution_bitcast_fusion
  399.0 0.2 fusion.10
  399.2 1.0 convolution_convert_fusion.1
  400.2 0.9 copy.51
  401.1 0.0 all-gather.3.cloned.1.call-update
  401.1 0.0 all-gather.5.cloned.1.call-start
  401.2 0.3 convolution_convert_fusion
  401.6 1.1 copy.50
  402.7 0.0 all-gather.5.cloned.1.call-update
  402.7 0.0 all-reduce.9.cloned.1.call-start
  402.8 0.1 eq.40
  402.9 54.6 %all-gather.3.cloned.1.call-done = bf16[256,8192]{1,0:T(8,128)(2,1)} async-done(((bf16[16,8192]{1,0:T(8,128)(2,1)}), bf16[256,8192]{1,0:T(8,128)(2,1)}) %all-gather.3.cloned.1.call-update) | async-done | bytes 4194320 | tf_op jit(solution)/shard_map/all_gather | solution.py:99
  457.4 57.9 %all-gather.5.cloned.1.call-done = bf16[512,8192]{1,0:T(8,128)(2,1)} async-done(((bf16[32,8192]{1,0:T(8,128)(2,1)}), bf16[512,8192]{1,0:T(8,128)(2,1)}) %all-gather.5.cloned.1.call-update) | async-done | bytes 8388624 | tf_op jit(solution)/shard_map/all_gather | solution.py:85
  515.3 7.2 %convolution_multiply_fusion.1 = f32[256,512]{1,0:T(8,128)S(1)} fusion(bf16[256,8192]{1,0:T(8,128)(2,1)} %all-gather.3.cloned.1.call-done, bf16[512,8192]{1,0:T(8,128)(2,1)} %all-gather.5.cloned.1.call-done), kind=kOutput, calls=%fused_computation.5 | convolution fusion | flops 2147614720 | bytes 13107200 | tf_op jit(solution)/shard_map/dot_general | solution.py:98
  522.5 0.4 convolution_multiply_fusion
  522.9 1.1 fusion
  524.0 0.6 dynamic-slice
  525.3 1.0 copy.37
  526.3 88.2 %all-reduce.9.cloned.1.call-done = bf16[256,128]{1,0:T(8,128)(2,1)} async-done(((bf16[256,128]{1,0:T(8,128)(2,1)}), bf16[256,128]{1,0:T(8,128)(2,1)}) %all-reduce.9.cloned.1.call-update) | async-done | bytes 65552
  614.5 1.3 bitcast_convert_fusion
  (29 shorter events, 0.2 us)
Async XLA Ops:
  7.2 30.0 %copy-start = (bf16[16,16,16,256]{3,2,1,0:T(8,128)(2,1)S(1)}, bf16[16,16,16,256]{3,2,1,0:T(8,128)(2,1)}, u32[]{:S(2)}) copy-start(bf16[16,16,16,256]{3,2,1,0:T(8,128)(2,1)} %param.9) | copy-start | bytes 6291460
  7.2 140.3 %reduce-scatter.2.cloned.1.call-start = ((), (), s32[]{:S(2)}) async-start(), calls=%async_computation.1 | async-start | bytes 13369344 | tf_op jit(solution)/shard_map/reduce_scatter | solution.py:54
  7.2 3.9 copy-start.2
  7.2 3.9 copy-start.5
  24.1 13.1 %copy-start.4 = (bf16[256,128]{1,0:T(8,128)(2,1)S(1)}, bf16[256,128]{1,0:T(8,128)(2,1)}, u32[]{:S(2)}) copy-start(bf16[256,128]{1,0:T(8,128)(2,1)} %param.13) | copy-start | bytes 196612
  37.1 1.6 copy-start.3
  65.0 337.8 %copy-start.7 = (s32[16,32]{1,0:T(8,128)S(1)}, s32[16,32]{1,0:T(8,128)}, u32[]{:S(2)}) copy-start(s32[16,32]{1,0:T(8,128)} %param.16) | copy-start | bytes 6148
  65.0 213.9 %all-reduce.5.cloned.1.call-start = ((), (), s32[]{:S(2)}) async-start(), calls=%async_computation.2 | async-start | bytes 131072 | tf_op jit(solution)/shard_map/psum | solution.py:66
  149.7 222.0 %all-reduce.7.cloned.1.call-start = ((), (), s32[]{:S(2)}) async-start(), calls=%async_computation.3 | async-start | bytes 131072 | tf_op jit(solution)/shard_map/psum | solution.py:66
  278.9 178.5 %all-gather.3.cloned.1.call-start = ((), (), s32[]{:S(2)}) async-start(), calls=%async_computation.4 | async-start | bytes 4456448 | tf_op jit(solution)/shard_map/all_gather | solution.py:99
  401.1 114.2 %all-gather.5.cloned.1.call-start = ((), (), s32[]{:S(2)}) async-start(), calls=%async_computation.5 | async-start | bytes 8912896 | tf_op jit(solution)/shard_map/all_gather | solution.py:85
  402.7 211.7 %all-reduce.9.cloned.1.call-start = ((), (), s32[]{:S(2)}) async-start(), calls=%async_computation.6 | async-start | bytes 131072
  402.9 119.6 %copy-start.6 = (s32[128,128]{1,0:T(8,128)S(1)}, s32[128,128]{1,0:T(8,128)}, u32[]{:S(2)}) copy-start(s32[128,128]{1,0:T(8,128)} %param.17) | copy-start | bytes 196612
  402.9 119.6 %copy-start.8 = (s32[1,256]{1,0:T(1,128)S(1)}, s32[1,256]{1,0:T(1,128)}, u32[]{:S(2)}) copy-start(s32[1,256]{1,0:T(1,128)} %param.15) | copy-start | bytes 3076
  402.9 121.1 %copy-start.9 = (u32[256]{0:T(256)S(1)}, u32[256]{0:T(256)}, u32[]{:S(2)}) copy-start(u32[256]{0:T(256)} %constant.124) | copy-start | bytes 3076
  515.3 100.4 %copy-start.1 = (bf16[16,16,16,256]{3,2,1,0:T(8,128)(2,1)S(1)}, bf16[16,16,16,256]{3,2,1,0:T(8,128)(2,1)}, u32[]{:S(2)}) copy-start(bf16[16,16,16,256]{3,2,1,0:T(8,128)(2,1)} %param.9) | copy-start | bytes 6291460
Sparse Core Ops, SparseCore 0:
  65.1 82.2 reduce-scatter.1
  150.3 100.1 all-reduce.4
  279.0 92.6 all-reduce.6
  401.2 56.1 all-gather.2
  459.7 55.5 all-gather.4
  524.1 90.3 all-reduce.8
